TPU v7x, 32 devices: a whole 2x2x4 slice. The times are simulated.
32 devices in a mesh: rows: 16 (over z, x, core), heads: 2 (over y).
Axes of the slice: x: 2, y: 2, z: 4, core: 2. Of those that a mesh axis runs over, the one named last changes fastest.
Arguments:
- queries: bfloat16 [32, 4, 32, 1024], P('rows', 'heads'), may hold values from -6 to 6
- keys: bfloat16 [32, 4, 32, 1024], P('rows', 'heads'), may hold values from -6 to 6
- values: bfloat16 [32, 4, 32, 1024], P('rows', 'heads'), may hold values from -6 to 6
- d_out: bfloat16 [32, 4, 32, 1024], P('rows', 'heads'), may hold values from -8 to 8
- bias: bfloat16 [4, 1024, 1024], P('heads', 'rows'), may hold values from -4 to 400, as said below
- w_bias: bfloat16 [128, 4], replicated, may hold values from -96 to 96
Outputs:
- d_queries: bfloat16 [32, 4, 32, 1024], P('rows', 'heads')
- d_keys: bfloat16 [32, 4, 32, 1024], P('rows', 'heads')
- d_values: bfloat16 [32, 4, 32, 1024], P('rows', 'heads')
- d_pair: bfloat16 [1024, 1024, 128], P('rows', 'heads')
Inputs may be any that keep to these rules, and one draw needn't show every extreme that they name: bias entries stay within the stated bounds.
All inputs are finite; a program needn't handle non-finite values.
Results may differ from a plain program's by a relative error of at most 0.0051.
Values may be sent and summed in bfloat16 or wider, within the bound.
A program may use at most 64 MiB of HBM per device.

v0:
```python
import math

import jax
import jax.numpy as jnp
from jax import lax
from jax.sharding import PartitionSpec as P


def block_terms(queries, keys, values, d_out, bias_block, start, scale):
    count = bias_block.shape[1]
    q_block = lax.dynamic_slice_in_dim(queries, start, count, 3)
    g_block = lax.dynamic_slice_in_dim(d_out, start, count, 3)
    bias_f = jnp.transpose(bias_block, (1, 0, 2)).astype(jnp.float32)
    scores = (
        jnp.einsum("rhdq,rhdk->rqhk", q_block, keys, preferred_element_type=jnp.float32) * scale
        + bias_f[None]
    )
    top = jnp.max(scores, axis=-1, keepdims=True)
    expo = jnp.exp(scores - top)
    probs = expo / jnp.sum(expo, axis=-1, keepdims=True)
    d_probs = jnp.einsum("rhdq,rhdk->rqhk", g_block, values, preferred_element_type=jnp.float32)
    d_scores = probs * (d_probs - jnp.sum(probs * d_probs, axis=-1, keepdims=True))
    return (q_block, g_block, probs, d_scores)


def block_grads(queries, keys, values, d_out, bias_block, start, scale, grads):
    grad_q, grad_k, grad_v = grads
    q_block, g_block, probs, d_scores = block_terms(
        queries, keys, values, d_out, bias_block, start, scale
    )
    d_low = d_scores.astype(jnp.bfloat16)
    probs_low = probs.astype(jnp.bfloat16)
    q_part = jnp.einsum("rqhk,rhdk->rhdq", d_low, keys, preferred_element_type=jnp.float32) * scale
    grad_q = lax.dynamic_update_slice(grad_q, q_part, (0, 0, 0, start))
    grad_k = (
        grad_k
        + jnp.einsum("rqhk,rhdq->rhdk", d_low, q_block, preferred_element_type=jnp.float32) * scale
    )
    grad_v = grad_v + jnp.einsum(
        "rqhk,rhdq->rhdk", probs_low, g_block, preferred_element_type=jnp.float32
    )
    return ((grad_q, grad_k, grad_v), jnp.sum(d_scores, axis=0))


def shards(queries, keys, values, d_out, bias, w_bias):
    row_count, head_count, depth, length = queries.shape
    scale = depth ** (-0.5)
    empty = jnp.zeros(queries.shape, jnp.float32)
    start_bias = jnp.zeros((length, head_count, length), jnp.float32)
    carry = (empty, empty, empty, start_bias)
    piece = lax.all_gather(bias, "rows", axis=1, tiled=True)
    grads = carry[:3]
    d_bias = carry[3]
    count = piece.shape[1]
    width = math.gcd(count, 64)

    def per_block(step, inner):
        grads_in, bias_in = inner
        first = step * width
        sub = lax.dynamic_slice_in_dim(piece, first, width, 1)
        grads_out, part_sum = block_grads(queries, keys, values, d_out, sub, first, scale, grads_in)
        bias_out = lax.dynamic_update_slice(bias_in, part_sum, (first, 0, 0))
        return (grads_out, bias_out)

    grads, d_bias = lax.fori_loop(0, count // width, per_block, (grads, d_bias))
    grad_q, grad_k, grad_v, d_bias = (grads[0], grads[1], grads[2], d_bias)
    owned = lax.psum_scatter(d_bias, "rows", scatter_dimension=0, tiled=True)
    weight_f = w_bias.astype(jnp.float32)
    every_head = lax.all_to_all(owned, "heads", split_axis=2, concat_axis=1, tiled=True)
    d_pair = jnp.einsum(
        "jhk,ch->jkc", every_head, weight_f, precision=lax.Precision.HIGHEST
    ).astype(jnp.bfloat16)
    return (
        grad_q.astype(jnp.bfloat16),
        grad_k.astype(jnp.bfloat16),
        grad_v.astype(jnp.bfloat16),
        d_pair,
    )


def solution(mesh):
    return jax.shard_map(
        shards,
        mesh=mesh,
        in_specs=(
            P("rows", "heads", None, None),
            P("rows", "heads", None, None),
            P("rows", "heads", None, None),
            P("rows", "heads", None, None),
            P("heads", "rows", None),
            P(),
        ),
        out_specs=(
            P("rows", "heads", None, None),
            P("rows", "heads", None, None),
            P("rows", "heads", None, None),
            P("rows", "heads", None),
        ),
        check_vma=False,
    )
```

profile of v0, /device:TPU:0, one launch (start us, length us, event | category | flops | bytes accessed | tf_op | source)
XLA Modules:
  0.0 459.5 jit_solution(6927943295869021733)
XLA Ops:
  8.0 55.4 %all-gather.2.cloned.1.call-done = bf16[2,1024,1024]{2,1,0:T(8,128)(2,1)} async-done(((bf16[2,64,1024]{2,1,0:T(8,128)(2,1)}), bf16[2,1024,1024]{2,1,0:T(8,128)(2,1)}) %all-gather.2.cloned.1.call-update) | async-done | bytes 4194320 | tf_op jit(solution)/shard_map/all_gather | solution.py:51
  64.1 5.6 %broadcast_in_dim.19.clone = f32[1024,2,1024]{2,1,0:T(2,128)} broadcast(f32[]{:T(128)} %constant.52.clone.1), dimensions={} | broadcast | bytes 8388612 | tf_op jit(solution)/shard_map/broadcast_in_dim | solution.py:49
  69.6 179.1 %while.20 = (s32[]{:T(128)}, bf16[2,2,32,1024]{3,2,1,0:T(8,128)(2,1)}, f32[2,2,32,1024]{3,2,1,0:T(8,128)S(1)}, f32[2,2,32,1024]{3,2,1,0:T(8,128)}, f32[1024,2,10...) while((s32[]{:T(128)}, ...), condition=%wide.region_5.0_spmd.clone, body=%wide.region_0.0_spmd.clone.sunk | while | flops 105793536 | bytes 13590237 | solution.py:65
  74.0 1.5 dynamic_update_slice.20
  76.6 2.5 convolution_add_fusion.2
  82.7 1.5 multiply_reduce_fusion.2
  84.7 2.1 dynamic_update_slice.20
  87.8 2.8 convolution_add_fusion.2
  94.2 1.5 multiply_reduce_fusion.2
  96.2 1.5 dynamic_update_slice.20
  98.8 2.8 convolution_add_fusion.2
  105.2 1.5 multiply_reduce_fusion.2
  107.2 2.1 dynamic_update_slice.20
  110.3 2.8 convolution_add_fusion.2
  118.7 1.5 dynamic_update_slice.20
  121.3 2.8 convolution_add_fusion.2
  127.6 1.5 multiply_reduce_fusion.2
  129.6 2.1 dynamic_update_slice.20
  132.8 2.8 convolution_add_fusion.2
  141.2 1.5 dynamic_update_slice.20
  143.7 2.8 convolution_add_fusion.2
  150.1 1.5 multiply_reduce_fusion.2
  152.1 2.1 dynamic_update_slice.20
  155.3 2.8 convolution_add_fusion.2
  163.6 1.5 dynamic_update_slice.20
  166.2 2.8 convolution_add_fusion.2
  172.6 1.5 multiply_reduce_fusion.2
  174.6 2.1 dynamic_update_slice.20
  177.7 2.8 convolution_add_fusion.2
  186.1 1.5 dynamic_update_slice.20
  188.7 2.8 convolution_add_fusion.2
  195.1 1.5 multiply_reduce_fusion.2
  197.1 2.1 dynamic_update_slice.20
  200.2 2.8 convolution_add_fusion.2
  208.6 1.5 dynamic_update_slice.20
  211.2 2.8 convolution_add_fusion.2
  217.5 1.5 multiply_reduce_fusion.2
  219.5 2.1 dynamic_update_slice.20
  222.7 2.8 convolution_add_fusion.2
  233.6 2.8 convolution_add_fusion.2
  241.9 1.7 dynamic_update_slice.20
  244.8 2.8 convolution_add_fusion.2
  250.6 166.9 %all-reduce.3.cloned.1.call-done = f32[1024,2,1024]{2,1,0:T(2,128)} async-done(((f32[1024,2,1024]{2,1,0:T(2,128)}), f32[1024,2,1024]{2,1,0:T(2,128)}) %all-reduce.3.cloned.1.call-update) | async-done | bytes 8388624
  419.2 1.8 reshape.14
  421.0 3.7 all-to-all-start
  426.2 6.5 %all-to-all-done = f32[2,1,65536]{2,1,0:T(1,128)S(1)} async-done(((f32[2,1,65536]{2,1,0:T(1,128)}), f32[2,1,65536]{2,1,0:T(1,128)S(1)}, u32[]{:S(2)}, u32[]{:S(2)}) %all-to-all-start) | async-done | bytes 524320 | tf_op jit(solution)/shard_map/all_to_all | solution.py:69
  433.2 2.3 reduce
  437.5 15.1 %convolution_convert_fusion = bf16[64,512,128]{2,1,0:T(8,128)(2,1)} fusion(f32[64,4,512]{2,1,0:T(4,128)S(1)} %all_to_all.16, bf16[128,4]{0,1:T(4,128)(2,1)S(1)} %copy-done), kind=kOutput, calls=%fused_computation.32 | convolution fusion | flops 205520896 | bytes 8913920 | tf_op jit(solution)/shard_map/jhk,ch->jkc/dot_general | solution.py:70
  (129 shorter events, 104.2 us)
Async XLA Ops:
  7.2 430.4 %copy-start = (bf16[128,4]{0,1:T(4,128)(2,1)S(1)}, bf16[128,4]{0,1:T(4,128)(2,1)}, u32[]{:S(2)}) copy-start(bf16[128,4]{0,1:T(4,128)(2,1)} %param.13) | copy-start | bytes 3076
  7.2 62.5 %copy-start.1 = (bf16[2,2,32,1024]{3,2,1,0:T(8,128)(2,1)S(1)}, bf16[2,2,32,1024]{3,2,1,0:T(8,128)(2,1)}, u32[]{:S(2)}) copy-start(bf16[2,2,32,1024]{3,2,1,0:T(8,128)(2,1)} %param.9) | copy-start | bytes 786436
  7.2 56.2 %all-gather.2.cloned.1.call-start = ((), (), s32[]{:S(2)}) async-start(), calls=%async_computation.1 | async-start | bytes 4456448 | tf_op jit(solution)/shard_map/all_gather | solution.py:51
  7.9 409.6 %all-reduce.3.cloned.1.call-start = ((), (), s32[]{:S(2)}) async-start(), calls=%async_computation.2 | async-start | bytes 16777216
  248.7 0.7 copy-start.3
  248.7 176.7 %copy-start.2 = (f32[2,2,32,1024]{3,2,1,0:T(8,128)S(1)}, f32[2,2,32,1024]{3,2,1,0:T(8,128)}, u32[]{:S(2)}) copy-start(f32[2,2,32,1024]{3,2,1,0:T(8,128)} %get-tuple-element.178) | copy-start | bytes 1572868
  421.0 11.7 %all-to-all-start = ((f32[2,1,65536]{2,1,0:T(1,128)}), f32[2,1,65536]{2,1,0:T(1,128)S(1)}, u32[]{:S(2)}, u32[]{:S(2)}) async-start(f32[2,1,65536]{2,1,0:T(1,128)} %reshape.14), calls=%async_computation | async-start | bytes 1048576 | tf_op jit(solution)/shard_map/all_to_all | solution.py:69
Sparse Core Ops, SparseCore 0:
  10.2 53.1 all-gather.1
  248.9 168.6 all-reduce.2
where the time goes:
time: 464 us; the launch traced here: 460 us
  waiting for transfers between devices  230 us (50%)
  matrix products  127 us (27%)
  local copies, waits for them, and re-layouts  60.7 us (13%)
  other arithmetic  23.6 us (5%)
  between operations  14.8 us (3%)
    unnamed x3, waiting for transfers between devices  168 us
    all_gather x1, waiting for transfers between devices, shards(): piece = lax.all_gather(bias, 'rows', axis=1, tiled=True)  55.4 us
    dot_general x16, matrix products, block_grads(): jnp.einsum('rqhk,rhdq->rhdk', probs_low, g_block, preferred_element_type=...  44.1 us
    dynamic_update_slice x16, local copies, waits for them, and re-layouts, block_grads(): grad_q = lax.dynamic_update_slice(grad_q, q_part, (0, 0, 0, start))  28.1 us
    dot_general x16, matrix products, block_terms(): jnp.einsum('rhdq,rhdk->rqhk', g_block, values, preferred_element_type=jnp...  23.6 us
    sub x16, matrix products, block_terms(): expo = jnp.exp(scores - top)  22.5 us
    dynamic_update_slice x16, local copies, waits for them, and re-layouts, per_block(): bias_out = lax.dynamic_update_slice(bias_in, part_sum, (first, 0, 0))  19.2 us
    dot_general x16, matrix products, block_grads(): jnp.einsum('rqhk,rhdq->rhdk', d_low, q_block, preferred_element_type=jnp....  17.2 us
  transfers between devices with their start and end apart: 3, of which 3 were waited for; matrix products, arithmetic and copies ran while one was open for 0% of the time, Pallas kernels for 0%

commit v1 on v0

v1 whole, which is shorter than its diff:
```python
import functools

import jax
import jax.numpy as jnp
from jax import lax
from jax.experimental import pallas as pl
from jax.experimental.pallas import tpu as pltpu
from jax.sharding import PartitionSpec as P

MESH = pl.DeviceIdType.MESH
GROUP = 4
BF16, F32 = jnp.bfloat16, jnp.float32


def xor(a, b, top):
    total, bit = 0, 1
    while bit < top:
        total = total + bit * lax.rem(lax.rem(lax.div(a, bit), 2) + lax.rem(lax.div(b, bit), 2), 2)
        bit *= 2
    return total


def attention_kernel(
    n, nh, q_ref, k_ref, v_ref, g_ref, bias_ref, dq_ref, dk_ref, dv_ref, eh_ref,
    q_t, g_t, k_t, dq_t, dk_acc, dv_acc, p_low, d_low, d_blk,
    bias_all, core_send, core_keep, core_recv, side_send, side_keep, side_recv,
    far_send, far_recv, own, fin, y_recv,
    zs, zr, xs, xr, as_, ar, bs, br, cs, cr, ss, sr, fs, fr, ys, yr,
):
    rows, heads, depth, length = q_ref.shape
    j_own = length // n
    blocks = n // GROUP
    steps = heads * blocks
    width = length // nh
    scale = depth ** (-0.5)
    me, hd = lax.axis_index("rows"), lax.axis_index("heads")
    core = lax.rem(me, 2)
    side = lax.rem(lax.div(me, 2), 2)
    far = lax.div(me, GROUP)
    core_peer = (me + 1 - 2 * core, hd)
    side_peer = (me + 2 - 4 * side, hd)

    def far_peer(i):
        return (xor(far, i, blocks) * GROUP + lax.rem(me, GROUP), hd)

    def step_of(t):
        h = lax.div(t, blocks)
        i = lax.rem(t, blocks)
        return h, i + lax.rem(h, 2) * (blocks - 1 - 2 * i)

    def remote(src, dst, send, recv, device):
        return pltpu.make_async_remote_copy(
            src_ref=src, dst_ref=dst, send_sem=send, recv_sem=recv, device_id=device, device_id_type=MESH
        )

    def bias_far(h, i):
        return remote(bias_ref.at[h], bias_all.at[h, i, side, core], zs.at[h, i], zr.at[h, i], far_peer(i))

    def bias_side(h, i):
        spot = bias_all.at[h, i, side, core]
        return remote(spot, spot, xs.at[h, i], xr.at[h, i], side_peer)

    def bias_core_a(h, i):
        spot = bias_all.at[h, i, side, core]
        return remote(spot, spot, as_.at[h, i], ar.at[h, i], core_peer)

    def bias_core_b(h, i):
        spot = bias_all.at[h, i, 1 - side, core]
        return remote(spot, spot, bs.at[h, i], br.at[h, i], core_peer)

    def sum_core(t):
        return remote(core_send.at[t], core_recv.at[t], cs.at[t], cr.at[t], core_peer)

    def sum_side(t):
        return remote(side_send.at[t], side_recv.at[t], ss.at[t], sr.at[t], side_peer)

    def sum_far(h, i):
        return remote(far_send.at[h, i], far_recv.at[h, i], fs.at[h, i], fr.at[h, i], far_peer(i))

    def head_copy(o, h):
        to = lax.rem(hd + o, nh)
        return remote(fin.at[to, h], y_recv.at[o - 1, h], ys.at[o - 1, h], yr.at[o - 1, h], (me, to))

    def stage_far(t):
        h, i = step_of(t)

        @pl.when(i != 0)
        def _():
            bias_far(h, i).wait_recv()

        bias_side(h, i).start()
        bias_core_a(h, i).start()

    def stage_side(t):
        h, i = step_of(t)
        bias_side(h, i).wait_recv()
        bias_core_b(h, i).start()

    def stage_core(t):
        h, i = step_of(t)
        bias_core_a(h, i).wait_recv()
        bias_core_b(h, i).wait_recv()

    def reduce_core(t):
        sum_core(t).wait_recv()
        side_send[t] = (core_keep[t, 1 - side] + core_recv[t, 1 - side].astype(F32)).astype(BF16)
        sum_side(t).start()
        side_keep[t] = core_keep[t, side] + core_recv[t, side].astype(F32)

    def reduce_side(t):
        h, i = step_of(t)
        sum_side(t).wait_recv()
        total = side_keep[t] + side_recv[t].astype(F32)

        @pl.when(i != 0)
        def _():
            far_send[h, i] = total.astype(BF16)
            sum_far(h, i).start()

        @pl.when(i == 0)
        def _():
            own[h] = total

    barrier = pltpu.get_barrier_semaphore()
    peers = [core_peer, side_peer]
    peers += [far_peer(i) for i in range(1, blocks)]
    peers += [(me, lax.rem(hd + o, nh)) for o in range(1, nh)]
    for peer in peers:
        pl.semaphore_signal(barrier, inc=1, device_id=peer, device_id_type=MESH)
    pl.semaphore_wait(barrier, len(peers))

    for h in range(heads):
        bias_all[h, 0, side, core] = bias_ref[h]
    stage_far(0)

    @pl.loop(0, steps)
    def _(t):
        h, i = step_of(t)

        @pl.when(i != 0)
        def _():
            bias_far(h, i).start()

    for r in range(rows):
        for h in range(heads):
            q_t[r, h] = q_ref[r, h].T
            g_t[r, h] = g_ref[r, h].T
            k_t[r, h] = k_ref[r, h].T
    dk_acc[...] = jnp.zeros_like(dk_acc)
    dv_acc[...] = jnp.zeros_like(dv_acc)
    stage_side(0)
    if steps > 1:
        stage_far(1)

    block = GROUP * j_own
    sub = min(block, 64)
    per_sub = sub // j_own if sub > j_own else 1
    sub = per_sub * j_own
    nn = (((1,), (0,)), ((), ()))
    tn = (((0,), (0,)), ((), ()))

    @pl.loop(0, steps)
    def _(t):
        h, i = step_of(t)

        @pl.when(t + 2 < steps)
        def _():
            stage_far(t + 2)

        @pl.when(t + 1 < steps)
        def _():
            stage_side(t + 1)

        stage_core(t)
        first = pl.multiple_of(xor(far, i, blocks) * block, block)

        @pl.loop(0, block // sub)
        def _(part):
            at = pl.multiple_of(part * sub, sub)
            pieces = []
            for u in range(per_sub):
                o = part * per_sub + u
                pieces.append(bias_all[h, i, lax.div(o, 2), lax.rem(o, 2)].astype(F32))
            b = pieces[0] if per_sub == 1 else jnp.concatenate(pieces, axis=0)
            total = None
            for r in range(rows):
                qb = q_t[r, h, pl.ds(first + at, sub), :]
                gb = g_t[r, h, pl.ds(first + at, sub), :]
                s = lax.dot_general(qb, k_ref[r, h], nn, preferred_element_type=F32) * scale + b
                e = jnp.exp(s - jnp.max(s, axis=-1, keepdims=True))
                inv = 1.0 / jnp.sum(e, axis=-1, keepdims=True)
                dp = lax.dot_general(gb, v_ref[r, h], nn, preferred_element_type=F32)
                p = e * inv
                delta = jnp.sum(p * dp, axis=-1, keepdims=True)
                ds = p * (dp - delta)
                p_low[r, pl.ds(at, sub), :] = p.astype(BF16)
                d_low[r, pl.ds(at, sub), :] = ds.astype(BF16)
                total = ds if total is None else total + ds
            for u in range(per_sub):
                o = part * per_sub + u
                d_blk[lax.div(o, 2), lax.rem(o, 2)] = total[u * j_own : (u + 1) * j_own]

        core_send[t] = d_blk[:, 1 - core].astype(BF16)
        sum_core(t).start()
        core_keep[t] = d_blk[:, core]
        for r in range(rows):
            qb = q_t[r, h, pl.ds(first, block), :]
            gb = g_t[r, h, pl.ds(first, block), :]
            dq_t[r, h, pl.ds(first, block), :] = lax.dot_general(d_low[r], k_t[r, h], nn, preferred_element_type=F32)
            dk_acc[r, h] += lax.dot_general(qb, d_low[r], tn, preferred_element_type=F32)
            dv_acc[r, h] += lax.dot_general(gb, p_low[r], tn, preferred_element_type=F32)

        @pl.when(t >= 1)
        def _():
            reduce_core(t - 1)

        @pl.when(t >= 2)
        def _():
            reduce_side(t - 2)

    def finish(h):
        @pl.loop(1, blocks)
        def _(i):
            sum_far(h, i).wait_recv()
            own[h] += far_recv[h, i].astype(F32)

        for y in range(nh):
            fin[y, h] = own[h, :, y * width : (y + 1) * width]
        for o in range(1, nh):
            head_copy(o, h).start()
        eh_ref[hd * heads + h] = fin[hd, h]

    reduce_core(steps - 1)
    if steps > 1:
        reduce_side(steps - 2)
    for h in range(heads - 1):
        finish(h)
    for r in range(rows):
        for h in range(heads):
            dq_ref[r, h] = (dq_t[r, h] * scale).T.astype(BF16)
            dk_ref[r, h] = (dk_acc[r, h] * scale).astype(BF16)
            dv_ref[r, h] = dv_acc[r, h].astype(BF16)
    reduce_side(steps - 1)
    finish(heads - 1)
    for h in range(heads):
        for o in range(1, nh):
            copy = head_copy(o, h)
            copy.wait_recv()
            eh_ref[lax.rem(hd + nh - o, nh) * heads + h] = y_recv[o - 1, h]
            copy.wait_send()

    @pl.loop(0, steps)
    def _(t):
        h, i = step_of(t)
        bias_side(h, i).wait_send()
        bias_core_a(h, i).wait_send()
        bias_core_b(h, i).wait_send()
        sum_core(t).wait_send()
        sum_side(t).wait_send()

        @pl.when(i != 0)
        def _():
            bias_far(h, i).wait_send()
            sum_far(h, i).wait_send()


def attention(n, nh, q, k, v, g, bias):
    rows, heads, depth, length = q.shape
    j_own = length // n
    blocks = n // GROUP
    steps = heads * blocks
    block = GROUP * j_own
    width = length // nh
    dma = pltpu.SemaphoreType.DMA
    vm = pltpu.VMEM
    grid2 = (heads, blocks)
    return pl.pallas_call(
        functools.partial(attention_kernel, n, nh),
        out_shape=[jax.ShapeDtypeStruct(q.shape, BF16)] * 3
        + [jax.ShapeDtypeStruct((nh * heads, j_own, width), F32)],
        in_specs=[pl.BlockSpec(memory_space=pltpu.VMEM)] * 5,
        out_specs=[pl.BlockSpec(memory_space=pltpu.VMEM)] * 4,
        scratch_shapes=[
            vm((rows, heads, length, depth), BF16),
            vm((rows, heads, length, depth), BF16),
            vm((rows, heads, length, depth), BF16),
            vm((rows, heads, length, depth), F32),
            vm(q.shape, F32),
            vm(q.shape, F32),
            vm((rows, block, length), BF16),
            vm((rows, block, length), BF16),
            vm((2, 2, j_own, length), F32),
            vm(grid2 + (2, 2, j_own, length), BF16),
            vm((steps, 2, j_own, length), BF16),
            vm((steps, 2, j_own, length), F32),
            vm((steps, 2, j_own, length), BF16),
            vm((steps, j_own, length), BF16),
            vm((steps, j_own, length), F32),
            vm((steps, j_own, length), BF16),
            vm(grid2 + (j_own, length), BF16),
            vm(grid2 + (j_own, length), BF16),
            vm((heads, j_own, length), F32),
            vm((nh, heads, j_own, width), F32),
            vm((max(nh - 1, 1), heads, j_own, width), F32),
        ]
        + [dma(grid2)] * 8
        + [dma((steps,))] * 4
        + [dma(grid2)] * 2
        + [dma((max(nh - 1, 1), heads))] * 2,
        compiler_params=pltpu.CompilerParams(
            collective_id=0, has_side_effects=True, vmem_limit_bytes=56 * 1024 * 1024
        ),
        name="attention",
    )(q, k, v, g, bias)


def pair_kernel(d_ref, w_ref, out_ref):
    heads, count, width = d_ref.shape
    d = d_ref[...].reshape(heads * count, width)
    high = d.astype(BF16)
    rest = d - high.astype(F32)
    mid = rest.astype(BF16)
    low = (rest - mid.astype(F32)).astype(BF16)
    parts = jnp.concatenate([high, mid, low], axis=0)
    channels = out_ref.shape[2]
    res = lax.dot_general(parts, w_ref[...], (((0,), (0,)), ((), ())), preferred_element_type=F32)
    for j in range(count):
        out_ref[j] = res[:, j * channels : (j + 1) * channels].astype(BF16)


def pair(every_head, w_bias):
    heads, j_own, width = every_head.shape
    channels = w_bias.shape[0]
    count = 8
    eye = jnp.eye(count, dtype=BF16)
    wide = (w_bias.T[:, None, None, :] * eye[None, :, :, None]).reshape(heads * count, count * channels)
    wide = jnp.concatenate([wide] * 3, axis=0)
    return pl.pallas_call(
        pair_kernel,
        grid=(j_own // count,),
        in_specs=[
            pl.BlockSpec((heads, count, width), lambda i: (0, i, 0)),
            pl.BlockSpec(wide.shape, lambda i: (0, 0)),
        ],
        out_specs=pl.BlockSpec((count, width, channels), lambda i: (i, 0, 0)),
        out_shape=jax.ShapeDtypeStruct((j_own, width, channels), BF16),
        name="pair",
    )(every_head, wide)


def solution(mesh):
    n, nh = mesh.shape["rows"], mesh.shape["heads"]

    def shards(queries, keys, values, d_out, bias, w_bias):
        dq, dk, dv, every_head = attention(n, nh, queries, keys, values, d_out, bias)
        return dq, dk, dv, pair(every_head, w_bias)

    spec = P("rows", "heads", None, None)
    return jax.shard_map(
        shards,
        mesh=mesh,
        in_specs=(spec, spec, spec, spec, P("heads", "rows", None), P()),
        out_specs=(spec, spec, spec, P("rows", "heads", None)),
        check_vma=False,
    )
```

time: 464 us -> 89.1 us (0.19)
  waiting for transfers between devices: 230 us -> 0 us
  matrix products: 127 us -> 0 us
  Pallas kernels: 0 us -> 84.4 us
  local copies, waits for them, and re-layouts: 60.7 us -> 2.12 us
  other arithmetic: 23.6 us -> 1.46 us
  between operations: 14.8 us -> 0.67 us
    unnamed x3 -> x0, waiting for transfers between devices: 168 us -> none
    dot_general x65 -> x0, matrix products: 104 us -> none  [the longest x16 44.1 us: block_grads(): jnp.einsum('rqhk,rhdq->rhdk', probs_low, g_block, preferred_element_type=...]
    pallas_call x0 -> x2, Pallas kernels: none -> 84.4 us  [the longest x1 76.7 us: attention(): pl.pallas_call(functools.partial(attention_kernel, n, nh), out_shape=[jax...]
    all_gather x1 -> x0, waiting for transfers between devices: 55.4 us -> none  [shards(): piece = lax.all_gather(bias, 'rows', axis=1, tiled=True)]
    dynamic_update_slice x32 -> x0, local copies, waits for them, and re-layouts: 47.3 us -> none  [the longest x16 28.1 us: block_grads(): grad_q = lax.dynamic_update_slice(grad_q, q_part, (0, 0, 0, start))]
    sub x16 -> x0, matrix products: 22.5 us -> none  [block_terms(): expo = jnp.exp(scores - top)]
    convert_element_type x18 -> x1, other arithmetic: 17.3 us -> 0.01 us  [pair(): eye = jnp.eye(count, dtype=BF16)]
    all_to_all x1 -> x0, waiting for transfers between devices: 6.54 us -> none  [shards(): lax.all_to_all(owned, 'heads', split_axis=2, concat_axis=1, tiled=True)]
  transfers between devices with their start and end apart: 3 -> 0, of which waited for: 3 -> 0; matrix products, arithmetic and copies ran while one was open for 0% -> 0% of each run, Pallas kernels for 0% -> 0%
where the time goes in v1:
time: 89.1 us; the launch traced here: 88.6 us
  Pallas kernels  84.4 us (95%)
  local copies, waits for them, and re-layouts  2.12 us (2%)
  other arithmetic  1.46 us (2%)
    pallas_call x1, Pallas kernels, attention(): pl.pallas_call(functools.partial(attention_kernel, n, nh), out_shape=[jax...  76.7 us
    pallas_call x1, Pallas kernels, pair(): pl.pallas_call(pair_kernel, grid=(j_own // count,), in_specs=[pl.BlockSpe...  7.66 us
    unnamed x9, local copies, waits for them, and re-layouts  2.12 us

profile of v1, /device:TPU:0, one launch (start us, length us, event | category | flops | bytes accessed | tf_op | source)
XLA Modules:
  0.0 88.6 jit_solution(9284381243034827675)
XLA Ops:
  0.6 0.8 multiply_bitcast_fusion
  1.4 0.7 pad_maximum_fusion.w_ref
  2.1 76.7 %attention.1 = (bf16[2,2,32,1024]{3,2,1,0:T(8,128)(2,1)}, bf16[2,2,32,1024]{3,2,1,0:T(8,128)(2,1)}, bf16[2,2,32,1024]{3,2,1,0:T(8,128)(2,1)}, f32[4,64,512]{2,1,0:T(8,128)}) custom-call(bf16[2,2,32,1024]{3,2,1,0:T(8,128)(2,1)} %q_ref.1, bf16[2,2,32,1024]{3,2,1,0:T(8,128)(2,1)} %k_ref.1, bf16[2,2,32,1024]{3,2,1,0:T(8,128)(2,1)} %v_ref.1, ...), custom_call_target="tpu_custom_call" | custom-call | tf_op jit(solution)/shard_map/attention/pallas_call | solution.py:277
  78.8 0.0 copy-start.2
  78.8 0.0 copy-start.1
  78.8 0.0 copy-start
  78.8 7.7 %pair.1 = bf16[64,512,128]{2,1,0:T(8,128)(2,1)} custom-call(f32[4,64,512]{2,1,0:T(8,128)} %get-tuple-element.11.d_ref, bf16[96,1024]{1,0:T(8,128)(2,1)} %pad_maximum_fusion.w_ref), custom_call_target="tpu_custom_call" | custom-call | tf_op jit(solution)/shard_map/pair/pallas_call | solution.py:338
  86.5 0.0 copy-done.2
  86.5 0.7 copy.13
  87.2 0.0 copy-done.1
  87.2 0.7 copy.14
  87.9 0.0 copy-done
  87.9 0.7 copy.15
  (1 shorter events, 0.0 us)
Async XLA Ops:
  78.8 7.7 %copy-start.2 = (bf16[2,2,32,1024]{3,2,1,0:T(8,128)(2,1)S(1)}, bf16[2,2,32,1024]{3,2,1,0:T(8,128)(2,1)}, u32[]{:S(2)}) copy-start(bf16[2,2,32,1024]{3,2,1,0:T(8,128)(2,1)} %get-tuple-element.16) | copy-start | bytes 786436
  78.8 8.4 %copy-start.1 = (bf16[2,2,32,1024]{3,2,1,0:T(8,128)(2,1)S(1)}, bf16[2,2,32,1024]{3,2,1,0:T(8,128)(2,1)}, u32[]{:S(2)}) copy-start(bf16[2,2,32,1024]{3,2,1,0:T(8,128)(2,1)} %get-tuple-element.17) | copy-start | bytes 786436
  78.8 9.1 %copy-start = (bf16[2,2,32,1024]{3,2,1,0:T(8,128)(2,1)S(1)}, bf16[2,2,32,1024]{3,2,1,0:T(8,128)(2,1)}, u32[]{:S(2)}) copy-start(bf16[2,2,32,1024]{3,2,1,0:T(8,128)(2,1)} %get-tuple-element.18) | copy-start | bytes 786436

commit v2 on v1

--- a/solution.py
+++ b/solution.py
@@ -8,6 +8,7 @@
 from jax.sharding import PartitionSpec as P
 
 MESH = pl.DeviceIdType.MESH
+AHEAD = 4
 GROUP = 4
 BF16, F32 = jnp.bfloat16, jnp.float32
 
@@ -24,7 +25,7 @@
     n, nh, q_ref, k_ref, v_ref, g_ref, bias_ref, dq_ref, dk_ref, dv_ref, eh_ref,
     q_t, g_t, k_t, dq_t, dk_acc, dv_acc, p_low, d_low, d_blk,
     bias_all, core_send, core_keep, core_recv, side_send, side_keep, side_recv,
-    far_send, far_recv, own, fin, y_recv,
+    far_send, far_recv, own, fin, fin_low, y_recv,
     zs, zr, xs, xr, as_, ar, bs, br, cs, cr, ss, sr, fs, fr, ys, yr,
 ):
     rows, heads, depth, length = q_ref.shape
@@ -79,7 +80,7 @@
 
     def head_copy(o, h):
         to = lax.rem(hd + o, nh)
-        return remote(fin.at[to, h], y_recv.at[o - 1, h], ys.at[o - 1, h], yr.at[o - 1, h], (me, to))
+        return remote(fin_low.at[to, h], y_recv.at[o - 1, h], ys.at[o - 1, h], yr.at[o - 1, h], (me, to))
 
     def stage_far(t):
         h, i = step_of(t)
@@ -127,24 +128,29 @@
     peers += [(me, lax.rem(hd + o, nh)) for o in range(1, nh)]
     for peer in peers:
         pl.semaphore_signal(barrier, inc=1, device_id=peer, device_id_type=MESH)
-    pl.semaphore_wait(barrier, len(peers))
-
-    for h in range(heads):
-        bias_all[h, 0, side, core] = bias_ref[h]
-    stage_far(0)
-
-    @pl.loop(0, steps)
-    def _(t):
-        h, i = step_of(t)
-
-        @pl.when(i != 0)
-        def _():
-            bias_far(h, i).start()
-
     for r in range(rows):
         for h in range(heads):
             q_t[r, h] = q_ref[r, h].T
             g_t[r, h] = g_ref[r, h].T
+    pl.semaphore_wait(barrier, len(peers))
+
+    for h in range(heads):
+        bias_all[h, 0, side, core] = bias_ref[h]
+    stage_far(0)
+
+    def send_far(t):
+        h, i = step_of(t)
+
+        @pl.when(i != 0)
+        def _():
+            bias_far(h, i).start()
+
+    ahead = min(AHEAD, steps)
+    for t in range(ahead):
+        send_far(jnp.int32(t))
+
+    for r in range(rows):
+        for h in range(heads):
             k_t[r, h] = k_ref[r, h].T
     dk_acc[...] = jnp.zeros_like(dk_acc)
     dv_acc[...] = jnp.zeros_like(dv_acc)
@@ -163,9 +169,9 @@
     def _(t):
         h, i = step_of(t)
 
-        @pl.when(t + 2 < steps)
-        def _():
-            stage_far(t + 2)
+        @pl.when(t + ahead < steps)
+        def _():
+            send_far(t + ahead)
 
         @pl.when(t + 1 < steps)
         def _():
@@ -203,6 +209,15 @@
         core_send[t] = d_blk[:, 1 - core].astype(BF16)
         sum_core(t).start()
         core_keep[t] = d_blk[:, core]
+
+        @pl.when((t == 0) & (steps > 2))
+        def _():
+            stage_far(t + 2)
+
+        @pl.when(t + 3 < steps)
+        def _():
+            stage_far(t + 3)
+
         for r in range(rows):
             qb = q_t[r, h, pl.ds(first, block), :]
             gb = g_t[r, h, pl.ds(first, block), :]
@@ -210,13 +225,11 @@
             dk_acc[r, h] += lax.dot_general(qb, d_low[r], tn, preferred_element_type=F32)
             dv_acc[r, h] += lax.dot_general(gb, p_low[r], tn, preferred_element_type=F32)
 
+        reduce_core(t)
+
         @pl.when(t >= 1)
         def _():
-            reduce_core(t - 1)
-
-        @pl.when(t >= 2)
-        def _():
-            reduce_side(t - 2)
+            reduce_side(t - 1)
 
     def finish(h):
         @pl.loop(1, blocks)
@@ -226,13 +239,11 @@
 
         for y in range(nh):
             fin[y, h] = own[h, :, y * width : (y + 1) * width]
+            fin_low[y, h] = own[h, :, y * width : (y + 1) * width].astype(BF16)
         for o in range(1, nh):
             head_copy(o, h).start()
         eh_ref[hd * heads + h] = fin[hd, h]
 
-    reduce_core(steps - 1)
-    if steps > 1:
-        reduce_side(steps - 2)
     for h in range(heads - 1):
         finish(h)
     for r in range(rows):
@@ -246,7 +257,7 @@
         for o in range(1, nh):
             copy = head_copy(o, h)
             copy.wait_recv()
-            eh_ref[lax.rem(hd + nh - o, nh) * heads + h] = y_recv[o - 1, h]
+            eh_ref[lax.rem(hd + nh - o, nh) * heads + h] = y_recv[o - 1, h].astype(F32)
             copy.wait_send()
 
     @pl.loop(0, steps)
@@ -301,7 +312,8 @@
             vm(grid2 + (j_own, length), BF16),
             vm((heads, j_own, length), F32),
             vm((nh, heads, j_own, width), F32),
-            vm((max(nh - 1, 1), heads, j_own, width), F32),
+            vm((nh, heads, j_own, width), BF16),
+            vm((max(nh - 1, 1), heads, j_own, width), BF16),
         ]
         + [dma(grid2)] * 8
         + [dma((steps,))] * 4
@@ -314,38 +326,54 @@
     )(q, k, v, g, bias)
 
 
-def pair_kernel(d_ref, w_ref, out_ref):
+def pair_kernel(d_ref, w_ref, q_in, k_in, v_in, q_out, k_out, v_out, out_ref, wide):
     heads, count, width = d_ref.shape
+    channels = out_ref.shape[2]
+
+    @pl.when(pl.program_id(0) == 0)
+    def _():
+        wide[...] = jnp.zeros_like(wide)
+        for part in range(wide.shape[0] // (heads * count)):
+            for h in range(heads):
+                for j in range(count):
+                    row = (part * heads + h) * count + j
+                    wide[row : row + 1, j * channels : (j + 1) * channels] = w_ref[h : h + 1].astype(F32)
+        q_out[...] = q_in[...]
+        k_out[...] = k_in[...]
+        v_out[...] = v_in[...]
+
     d = d_ref[...].reshape(heads * count, width)
     high = d.astype(BF16)
     rest = d - high.astype(F32)
     mid = rest.astype(BF16)
     low = (rest - mid.astype(F32)).astype(BF16)
     parts = jnp.concatenate([high, mid, low], axis=0)
-    channels = out_ref.shape[2]
-    res = lax.dot_general(parts, w_ref[...], (((0,), (0,)), ((), ())), preferred_element_type=F32)
+    res = lax.dot_general(parts, wide[...].astype(BF16), (((0,), (0,)), ((), ())), preferred_element_type=F32)
     for j in range(count):
         out_ref[j] = res[:, j * channels : (j + 1) * channels].astype(BF16)
 
 
-def pair(every_head, w_bias):
+def pair(every_head, w_bias, grads):
     heads, j_own, width = every_head.shape
     channels = w_bias.shape[0]
     count = 8
-    eye = jnp.eye(count, dtype=BF16)
-    wide = (w_bias.T[:, None, None, :] * eye[None, :, :, None]).reshape(heads * count, count * channels)
-    wide = jnp.concatenate([wide] * 3, axis=0)
+    whole = pl.BlockSpec(grads[0].shape, lambda i: (0, 0, 0, 0))
     return pl.pallas_call(
         pair_kernel,
         grid=(j_own // count,),
         in_specs=[
             pl.BlockSpec((heads, count, width), lambda i: (0, i, 0)),
-            pl.BlockSpec(wide.shape, lambda i: (0, 0)),
+            pl.BlockSpec((heads, channels), lambda i: (0, 0)),
+            whole,
+            whole,
+            whole,
         ],
-        out_specs=pl.BlockSpec((count, width, channels), lambda i: (i, 0, 0)),
-        out_shape=jax.ShapeDtypeStruct((j_own, width, channels), BF16),
+        out_specs=[whole] * 3 + [pl.BlockSpec((count, width, channels), lambda i: (i, 0, 0))],
+        out_shape=[jax.ShapeDtypeStruct(grads[0].shape, BF16)] * 3
+        + [jax.ShapeDtypeStruct((j_own, width, channels), BF16)],
+        scratch_shapes=[pltpu.VMEM((3 * heads * count, count * channels), F32)],
         name="pair",
-    )(every_head, wide)
+    )(every_head, w_bias.T, *grads)
 
 
 def solution(mesh):
@@ -353,7 +381,7 @@
 
     def shards(queries, keys, values, d_out, bias, w_bias):
         dq, dk, dv, every_head = attention(n, nh, queries, keys, values, d_out, bias)
-        return dq, dk, dv, pair(every_head, w_bias)
+        return tuple(pair(every_head, w_bias, (dq, dk, dv)))
 
     spec = P("rows", "heads", None, None)
     return jax.shard_map(

time: 89.1 us -> 81.7 us (0.917)
  Pallas kernels: 84.4 us -> 80.6 us
  local copies, waits for them, and re-layouts: 2.12 us -> 0 us
  other arithmetic: 1.46 us -> 0 us
    pallas_call x1, Pallas kernels: 76.7 us -> 72.7 us  [attention(): pl.pallas_call(functools.partial(attention_kernel, n, nh), out_shape=[jax...]
    unnamed x9 -> x0, local copies, waits for them, and re-layouts: 2.12 us -> none
where the time goes in v2:
time: 81.7 us; the launch traced here: 81.2 us
  Pallas kernels  80.6 us (99%)
    pallas_call x1, Pallas kernels, attention(): pl.pallas_call(functools.partial(attention_kernel, n, nh), out_shape=[jax...  72.7 us
    pallas_call x1, Pallas kernels, pair(): pl.pallas_call(pair_kernel, grid=(j_own // count,), in_specs=[pl.BlockSpe...  7.9 us

profile of v2, /device:TPU:0, one launch (start us, length us, event | category | flops | bytes accessed | tf_op | source)
XLA Modules:
  0.0 81.2 jit_solution(9258958701589130416)
XLA Ops:
  0.6 72.7 %attention.1 = (bf16[2,2,32,1024]{3,2,1,0:T(8,128)(2,1)}, bf16[2,2,32,1024]{3,2,1,0:T(8,128)(2,1)}, bf16[2,2,32,1024]{3,2,1,0:T(8,128)(2,1)}, f32[4,64,512]{2,1,0:T(8,128)}) custom-call(bf16[2,2,32,1024]{3,2,1,0:T(8,128)(2,1)} %q_ref.1, bf16[2,2,32,1024]{3,2,1,0:T(8,128)(2,1)} %k_ref.1, bf16[2,2,32,1024]{3,2,1,0:T(8,128)(2,1)} %v_ref.1, ...), custom_call_target="tpu_custom_call" | custom-call | tf_op jit(solution)/shard_map/attention/pallas_call | solution.py:288
  73.3 7.9 %pair.1 = (bf16[2,2,32,1024]{3,2,1,0:T(8,128)(2,1)}, bf16[2,2,32,1024]{3,2,1,0:T(8,128)(2,1)}, bf16[2,2,32,1024]{3,2,1,0:T(8,128)(2,1)}, bf16[64,512,128]{2,1,0:T(8,128)(2,1)}) custom-call(f32[4,64,512]{2,1,0:T(8,128)} %get-tuple-element.8.d_ref, bf16[4,128]{1,0:T(4,128)(2,1)} %bitcast.1, bf16[2,2,32,1024]{3,2,1,0:T(8,128)(2,1)} %get-tuple-element.9.q_in, ...), custom_call_target="tpu_custom_call" | custom-call | tf_op jit(solution)/shard_map/pair/pallas_call | solution.py:361

commit v3 on v2

--- a/solution.py
+++ b/solution.py
@@ -88,9 +88,8 @@
         @pl.when(i != 0)
         def _():
             bias_far(h, i).wait_recv()
-
-        bias_side(h, i).start()
-        bias_core_a(h, i).start()
+            bias_side(h, i).start()
+            bias_core_a(h, i).start()
 
     def stage_side(t):
         h, i = step_of(t)
@@ -136,7 +135,9 @@
 
     for h in range(heads):
         bias_all[h, 0, side, core] = bias_ref[h]
-    stage_far(0)
+    for h in range(heads):
+        bias_side(h, 0).start()
+        bias_core_a(h, 0).start()
 
     def send_far(t):
         h, i = step_of(t)
@@ -356,7 +357,7 @@
 def pair(every_head, w_bias, grads):
     heads, j_own, width = every_head.shape
     channels = w_bias.shape[0]
-    count = 8
+    count = min(16, j_own)
     whole = pl.BlockSpec(grads[0].shape, lambda i: (0, 0, 0, 0))
     return pl.pallas_call(
         pair_kernel,

time: 81.7 us -> 78.7 us (0.963)
  Pallas kernels: 80.6 us -> 77.9 us
    pallas_call x1, Pallas kernels: 72.7 us -> 71.2 us  [attention(): pl.pallas_call(functools.partial(attention_kernel, n, nh), out_shape=[jax...]
    pallas_call x1, Pallas kernels: 7.9 us -> 6.64 us  [pair(): pl.pallas_call(pair_kernel, grid=(j_own // count,), in_specs=[pl.BlockSpe...]
where the time goes in v3:
time: 78.7 us; the launch traced here: 78.5 us
  Pallas kernels  77.9 us (99%)
    pallas_call x1, Pallas kernels, attention(): pl.pallas_call(functools.partial(attention_kernel, n, nh), out_shape=[jax...  71.2 us
    pallas_call x1, Pallas kernels, pair(): pl.pallas_call(pair_kernel, grid=(j_own // count,), in_specs=[pl.BlockSpe...  6.64 us

profile of v3, /device:TPU:0, one launch (start us, length us, event | category | flops | bytes accessed | tf_op | source)
XLA Modules:
  0.0 78.5 jit_solution(16983829786625732259)
XLA Ops:
  0.6 71.2 %attention.1 = (bf16[2,2,32,1024]{3,2,1,0:T(8,128)(2,1)}, bf16[2,2,32,1024]{3,2,1,0:T(8,128)(2,1)}, bf16[2,2,32,1024]{3,2,1,0:T(8,128)(2,1)}, f32[4,64,512]{2,1,0:T(8,128)}) custom-call(bf16[2,2,32,1024]{3,2,1,0:T(8,128)(2,1)} %q_ref.1, bf16[2,2,32,1024]{3,2,1,0:T(8,128)(2,1)} %k_ref.1, bf16[2,2,32,1024]{3,2,1,0:T(8,128)(2,1)} %v_ref.1, ...), custom_call_target="tpu_custom_call" | custom-call | tf_op jit(solution)/shard_map/attention/pallas_call | solution.py:289
  71.9 6.6 %pair.1 = (bf16[2,2,32,1024]{3,2,1,0:T(8,128)(2,1)}, bf16[2,2,32,1024]{3,2,1,0:T(8,128)(2,1)}, bf16[2,2,32,1024]{3,2,1,0:T(8,128)(2,1)}, bf16[64,512,128]{2,1,0:T(8,128)(2,1)}) custom-call(f32[4,64,512]{2,1,0:T(8,128)} %get-tuple-element.8.d_ref, bf16[4,128]{1,0:T(4,128)(2,1)} %bitcast.1, bf16[2,2,32,1024]{3,2,1,0:T(8,128)(2,1)} %get-tuple-element.9.q_in, ...), custom_call_target="tpu_custom_call" | custom-call | tf_op jit(solution)/shard_map/pair/pallas_call | solution.py:362
